TPU v7x, 32 devices: a whole 2x2x4 slice. The times are simulated.
32 devices in a mesh: gx: 8 (over z, core), gy: 4 (over y, x).
Axes of the slice: x: 2, y: 2, z: 4, core: 2. Of those that a mesh axis runs over, the one named last changes fastest.
Arguments:
- init_re: float32 [1, 256, 4096], P(None, 'gx', 'gy'), may hold values from -6 to 6
- init_im: float32 [1, 256, 4096], P(None, 'gx', 'gy'), may hold values from -6 to 6
- onsite: float32 [256, 4096], P('gx', 'gy'), may hold values from -0.9 to 0.9
- bond_x: int32 [256, 4096], P('gx', 'gy'), may hold values from 0 to 15
- bond_y: int32 [256, 4096], P('gx', 'gy'), may hold values from 0 to 15
- hop_table: float32 [16], replicated, may hold values from 1.4 to 1.6
- centre: int32 [1, 2], replicated, may hold values from 0 to 255
- duration: float32 [1], replicated, may hold values from 0.55 to 0.6
Outputs:
- out_re: float32 [1, 256, 4096], P(None, 'gx', 'gy')
- out_im: float32 [1, 256, 4096], P(None, 'gx', 'gy')
- term_norms: float32 [2, 8, 1], replicated
All inputs are finite; a program needn't handle non-finite values.
Results may differ from a plain program's by a relative error of at most 0.0003.
Values sent between devices are 32-bit elements; how exact they have to be, the bound alone decides.
A program may use at most 64 MiB of HBM per device.

v0:
```python
import math
import jax
import jax.numpy as jnp
from jax import lax
from jax.sharding import PartitionSpec as P

TERMS = 8
STEPS = 2
SPECTRAL = 7.5
epsilon = 1e-06


def padded(block, sides, width):
    for axis, dim in sides:
        count = lax.axis_size(axis)
        forward = [(i, i + 1) for i in range(count - 1)]
        forward.append((count - 1, 0))
        backward = [(target, source) for source, target in forward]
        low = lax.ppermute(
            lax.slice_in_dim(block, block.shape[dim] - width, None, axis=dim), axis, forward
        )
        high = lax.ppermute(lax.slice_in_dim(block, 0, width, axis=dim), axis, backward)
        block = jnp.concatenate([low, block, high], axis=dim)
    return block


def bessel_weights(duration):
    argument = duration[0] * SPECTRAL
    halved = argument * 0.5
    weights = []
    for degree in range(TERMS):
        series = halved**degree / math.factorial(degree)
        summed = series
        for counter in range(1, 24):
            series = series * -(halved * halved) / (counter * (counter + degree))
            summed = summed + series
        weights.append(summed if degree == 0 else 2.0 * summed)
    return weights


def rotated(degree, real_part, imag_part):
    quarter = degree % 4
    if quarter == 0:
        return (real_part, imag_part)
    if quarter == 1:
        return (imag_part, -real_part)
    if quarter == 2:
        return (-real_part, -imag_part)
    return (-imag_part, real_part)


def falloff(positions, centres, extent):
    distance = jnp.mod(positions[None, :] - centres[:, None], extent)
    distance = jnp.minimum(distance, extent - distance).astype(jnp.float32)
    return distance * distance * (4.5 / (extent * extent))


def shrink(tensor, margin):
    if margin == 0:
        return tensor
    return tensor[..., margin : tensor.shape[-2] - margin, margin : tensor.shape[-1] - margin]


def apply_wide(grid_field, coeffs):
    potential = coeffs[0]
    hop_rows = coeffs[1]
    hop_cols = coeffs[2]
    result = potential[1:-1, 1:-1] * grid_field[..., 1:-1, 1:-1]
    result = result - hop_rows[1:-1, 1:-1] * grid_field[..., 2:, 1:-1]
    result = result - hop_rows[:-2, 1:-1] * grid_field[..., :-2, 1:-1]
    result = result - hop_cols[1:-1, 1:-1] * grid_field[..., 1:-1, 2:]
    result = result - hop_cols[1:-1, :-2] * grid_field[..., 1:-1, :-2]
    return result * (1.0 / SPECTRAL)


def per_device(init_re, init_im, onsite, bond_x, bond_y, hop_table, centre, duration):
    packets, rows_local, cols_local = init_re.shape
    rows_total = rows_local * lax.axis_size("gx")
    cols_total = cols_local * lax.axis_size("gy")
    cell_count = rows_total * cols_total
    classes = hop_table.shape[0]
    selector = jnp.arange(classes, dtype=jnp.int32)[:, None, None]
    table_column = hop_table[:, None, None]
    hop_down = jnp.sum(jnp.where(bond_x[None] == selector, table_column, 0.0), axis=0)
    hop_right = jnp.sum(jnp.where(bond_y[None] == selector, table_column, 0.0), axis=0)
    weights = bessel_weights(duration)
    row_index = lax.axis_index("gx") * rows_local + lax.iota(jnp.int32, rows_local)
    col_index = lax.axis_index("gy") * cols_local + lax.iota(jnp.int32, cols_local)
    row_fall = falloff(row_index, centre[:, 0], rows_total)
    col_fall = falloff(col_index, centre[:, 1], cols_total)
    envelope = jnp.exp(-(row_fall[:, :, None] + col_fall[:, None, :]))
    packet_state = jnp.stack([init_re * envelope, init_im * envelope])
    reach = TERMS - 1
    coeffs = padded(jnp.stack([onsite, hop_down, hop_right]), (("gx", 1), ("gy", 2)), reach)
    norm_rows = []
    for repeat in range(STEPS):
        current = padded(packet_state, (("gx", 2), ("gy", 3)), reach)
        margin = reach
        previous = current
        previous_margin = reach
        chebyshev = [packet_state]
        for chebyshev_degree in range(1, TERMS):
            applied = apply_wide(current, shrink(coeffs, reach - margin))
            if chebyshev_degree == 1:
                following = applied
            else:
                following = 2.0 * applied - shrink(previous, previous_margin - margin + 1)
            previous, previous_margin = (current, margin)
            current = following
            margin = margin - 1
            chebyshev.append(shrink(following, margin))
        accumulate = weights[0] * packet_state
        for degree in range(1, TERMS):
            real_rot, imag_rot = rotated(degree, chebyshev[degree][0], chebyshev[degree][1])
            accumulate = accumulate + weights[degree] * jnp.stack([real_rot, imag_rot])
        term_local = jnp.stack([jnp.sum(vector * vector, axis=(0, 2, 3)) for vector in chebyshev])
        state_local = jnp.sum(accumulate * accumulate, axis=(0, 2, 3))
        term_total, state_total = lax.psum((term_local, state_local), ("gx", "gy"))
        norm_rows.append(term_total / cell_count)
        rescale = lax.rsqrt(state_total / cell_count + epsilon)
        packet_state = accumulate * rescale[None, :, None, None]
    return (packet_state[0], packet_state[1], jnp.stack(norm_rows))


def solution(mesh):
    return jax.shard_map(
        per_device,
        mesh=mesh,
        in_specs=(
            P(None, "gx", "gy"),
            P(None, "gx", "gy"),
            P("gx", "gy"),
            P("gx", "gy"),
            P("gx", "gy"),
            P(),
            P(),
            P(),
        ),
        out_specs=(P(None, "gx", "gy"), P(None, "gx", "gy"), P()),
        check_vma=False,
    )
```

profile of v0, /device:TPU:0, one launch (start us, length us, event | category | flops | bytes accessed | tf_op | source)
XLA Modules:
  0.0 153.5 jit_solution(4384548073286884623)
XLA Ops:
  0.7 1.3 fusion.128
  2.6 0.7 fusion.97
  3.3 1.1 multiply_bitcast_fusion
  5.0 4.1 %collective-permute-start.5 = (f32[2,1,7,1024]{3,2,1,0:T(8,128)S(1)}, f32[2,1,7,1024]{3,2,1,0:T(8,128)S(1)}, u32[]{:S(2)}, u32[]{:S(2)}) collective-permute-start(f32[2,1,7,1024]{3,2,1,0:T(8,128)S(1)} %get-tuple-element.80), channel_id=1, source_target_pairs={{4,0},{8,4},{12,8},{16,12},{20,16},{24,20},{28,24},{0,28},{5,1},{9... | collective-permute-start | bytes 172040 | tf_op jit(solution)/shard_map/ppermute | solution.py:22
  9.7 3.5 %collective-permute-start.1 = (f32[3,7,1024]{2,1,0:T(8,128)S(1)}, f32[3,7,1024]{2,1,0:T(8,128)S(1)}, u32[]{:S(2)}, u32[]{:S(2)}) collective-permute-start(f32[3,7,1024]{2,1,0:T(8,128)S(1)} %get-tuple-element.52), channel_id=1, source_target_pairs={{4,0},{8,4},{12,8},{16,12},{20,16},{24,20},{28,24},{0,28},{5,1},{9... | collective-permute-start | bytes 258056 | tf_op jit(solution)/shard_map/ppermute | solution.py:22
  14.5 0.7 multiply_reduce_fusion.9
  16.0 3.4 %collective-permute-start.3 = (f32[3,46,7]{2,1,0:T(8,128)S(1)}, f32[3,46,7]{2,1,0:T(8,128)S(1)}, u32[]{:S(2)}, u32[]{:S(2)}) collective-permute-start(f32[3,46,7]{2,1,0:T(8,128)S(1)} %get-tuple-element.39), channel_id=1, source_target_pairs={{1,0},{2,1},{3,2},{0,3},{5,4},{6,5},{7,6},{4,7},{9,8},{10,9},{11,1... | collective-permute-start | bytes 11600 | tf_op jit(solution)/shard_map/ppermute | solution.py:22
  19.4 2.9 %collective-permute-start.7 = (f32[2,1,46,7]{3,2,1,0:T(8,128)S(1)}, f32[2,1,46,7]{3,2,1,0:T(8,128)S(1)}, u32[]{:S(2)}, u32[]{:S(2)}) collective-permute-start(f32[2,1,46,7]{3,2,1,0:T(8,128)S(1)} %get-tuple-element.53), channel_id=1, source_target_pairs={{1,0},{2,1},{3,2},{0,3},{5,4},{6,5},{7,6},{4,7},{9,8},{10,9},{11,1... | collective-permute-start | bytes 7736 | tf_op jit(solution)/shard_map/ppermute | solution.py:22
  22.4 1.8 %collective-permute-done.7 = f32[2,1,46,7]{3,2,1,0:T(8,128)S(1)} collective-permute-done((f32[2,1,46,7]{3,2,1,0:T(8,128)S(1)}, f32[2,1,46,7]{3,2,1,0:T(8,128)S(1)}, u32[]{:S(2)}, u32[]{:S(2)}) %collective-permute-start.7) | collective-permute-done | bytes 2608 | tf_op jit(solution)/shard_map/ppermute | solution.py:22
  24.2 3.2 %collective-permute-done.6 = f32[2,1,46,7]{3,2,1,0:T(8,128)S(1)} collective-permute-done((f32[2,1,46,7]{3,2,1,0:T(8,128)S(1)}, f32[2,1,46,7]{3,2,1,0:T(8,128)S(1)}, u32[]{:S(2)}, u32[]{:S(2)}) %collective-permute-start.6) | collective-permute-done | bytes 2608 | tf_op jit(solution)/shard_map/ppermute | solution.py:19
  30.3 0.8 fusion.65
  32.3 0.8 fusion.64
  38.8 1.1 multiply_reduce_fusion.5
  39.9 0.9 multiply_reduce_fusion.11
  40.8 37.0 %psum.28 = f32[1]{0:T(128)} all-reduce(f32[1]{0:T(128)} %bitcast.29), channel_id=1, replica_groups=mesh['gx'=8,'gy'=4] {'gx','gy'}, use_global_device_ids=true, to_apply=%region_3.4 | all-reduce | flops 1 | bytes 8 | tf_op jit(solution)/shard_map/psum | solution.py:118
  78.5 0.7 multiply_reduce_fusion.4
  79.3 3.5 %collective-permute-start.9 = (f32[2,1,7,1024]{3,2,1,0:T(8,128)S(1)}, f32[2,1,7,1024]{3,2,1,0:T(8,128)S(1)}, u32[]{:S(2)}, u32[]{:S(2)}) collective-permute-start(f32[2,1,7,1024]{3,2,1,0:T(8,128)S(1)} %get-tuple-element.76), channel_id=1, source_target_pairs={{4,0},{8,4},{12,8},{16,12},{20,16},{24,20},{28,24},{0,28},{5,1},{9... | collective-permute-start | bytes 172040 | tf_op jit(solution)/shard_map/ppermute | solution.py:22
  82.8 0.7 fusion.63
  83.5 1.2 collective-permute-done.8
  84.9 2.5 %collective-permute-start.11 = (f32[2,1,46,7]{3,2,1,0:T(8,128)S(1)}, f32[2,1,46,7]{3,2,1,0:T(8,128)S(1)}, u32[]{:S(2)}, u32[]{:S(2)}) collective-permute-start(f32[2,1,46,7]{3,2,1,0:T(8,128)S(1)} %get-tuple-element.49), channel_id=1, source_target_pairs={{1,0},{2,1},{3,2},{0,3},{5,4},{6,5},{7,6},{4,7},{9,8},{10,9},{11,1... | collective-permute-start | bytes 7736 | tf_op jit(solution)/shard_map/ppermute | solution.py:22
  87.4 0.8 multiply_reduce_fusion.8
  88.1 5.1 %stack.171 = f32[8,1]{0,1:T(1,128)S(1)} concatenate(f32[1,1]{0,1:T(1,128)} %bitcast.35, f32[1,1]{0,1:T(1,128)} %bitcast.36, f32[1,1]{0,1:T(1,128)} %bitcast.37, f32[1,1]{0,1:T(1,128)} %bitcast.38, f32[1,1]{0,1:T(1,128)} %bitcast.39, f32[1,1]{0,1:T(1,128)} %bitcast.40, f32[1,1]{0,1:T(1,128)} %bitcast.41, f32[1,1]{0,1:T(1,128)} %bitcast.42), dimensions={0} | concatenate | bytes 64 | tf_op jit(solution)/shard_map/stack | solution.py:116
  93.9 1.1 concatenate.135
  95.5 0.8 fusion.62
  97.0 0.8 fusion.61
  98.4 0.8 fusion.60
  99.8 0.8 multiply_reduce_fusion.3
  103.6 1.0 multiply_reduce_fusion
  105.1 5.2 %stack.181 = f32[8,1]{0,1:T(1,128)S(1)} concatenate(f32[1,1]{0,1:T(1,128)} %bitcast.44, f32[1,1]{0,1:T(1,128)} %bitcast.45, f32[1,1]{0,1:T(1,128)} %bitcast.46, f32[1,1]{0,1:T(1,128)} %bitcast.47, f32[1,1]{0,1:T(1,128)} %bitcast.48, f32[1,1]{0,1:T(1,128)} %bitcast.49, f32[1,1]{0,1:T(1,128)} %bitcast.50, f32[1,1]{0,1:T(1,128)} %bitcast.51), dimensions={0} | concatenate | bytes 64 | tf_op jit(solution)/shard_map/stack | solution.py:116
  110.3 0.8 multiply_reduce_fusion.10
  111.1 40.4 %all-reduce = (f32[1]{0:T(128)}, f32[8,1]{0,1:T(1,128)S(1)}, f32[8,1]{0,1:T(1,128)S(1)}) all-reduce(f32[1]{0:T(128)} %bitcast.31, f32[8,1]{0,1:T(1,128)S(1)} %stack.181, f32[8,1]{0,1:T(1,128)S(1)} %stack.171), channel_id=1, replica_groups=mesh['gx'=8,'gy'=4] {'gx','gy'}, use_global_device_ids=true, to_apply=%region_5.6 | all-reduce | flops 17 | bytes 136 | tf_op jit(solution)/shard_map/psum | solution.py:118
  152.2 0.7 slice_bitcast_fusion.21
  (187 shorter events, 19.0 us)
Async XLA Ops:
  0.6 8.4 %copy-start.54 = (f32[16]{0:T(128)S(1)}, f32[16]{0:T(128)}, u32[]{:S(2)}) copy-start(f32[16]{0:T(128)} %param.13) | copy-start | bytes 196
  0.6 8.4 %copy-start.52 = (s32[32,1024]{1,0:T(8,128)S(1)}, s32[32,1024]{1,0:T(8,128)}, u32[]{:S(2)}) copy-start(s32[32,1024]{1,0:T(8,128)} %param.12) | copy-start | bytes 393220
  0.7 8.4 %copy-start.51 = (s32[32,1024]{1,0:T(8,128)S(1)}, s32[32,1024]{1,0:T(8,128)}, u32[]{:S(2)}) copy-start(s32[32,1024]{1,0:T(8,128)} %param.11) | copy-start | bytes 393220
  3.3 6.3 %copy-start.50 = (f32[32,1024]{1,0:T(8,128)S(1)}, f32[32,1024]{1,0:T(8,128)}, u32[]{:S(2)}) copy-start(f32[32,1024]{1,0:T(8,128)} %param.10) | copy-start | bytes 393220
  4.4 10.8 %collective-permute-start.4 = (f32[2,1,7,1024]{3,2,1,0:T(8,128)S(1)}, f32[2,1,7,1024]{3,2,1,0:T(8,128)S(1)}, u32[]{:S(2)}, u32[]{:S(2)}) collective-permute-start(f32[2,1,7,1024]{3,2,1,0:T(8,128)S(1)} %get-tuple-element.79), channel_id=1, source_target_pairs={{0,4},{4,8},{8,12},{12,16},{16,20},{20,24},{24,28},{28,0},{1,5},{5... | collective-permute-start | bytes 172040 | tf_op jit(solution)/shard_map/ppermute | solution.py:19
  5.0 10.3 %collective-permute-start.5 = (f32[2,1,7,1024]{3,2,1,0:T(8,128)S(1)}, f32[2,1,7,1024]{3,2,1,0:T(8,128)S(1)}, u32[]{:S(2)}, u32[]{:S(2)}) collective-permute-start(f32[2,1,7,1024]{3,2,1,0:T(8,128)S(1)} %get-tuple-element.80), channel_id=1, source_target_pairs={{4,0},{8,4},{12,8},{16,12},{20,16},{24,20},{28,24},{0,28},{5,1},{9... | collective-permute-start | bytes 172040 | tf_op jit(solution)/shard_map/ppermute | solution.py:22
  9.6 6.2 %collective-permute-start = (f32[3,7,1024]{2,1,0:T(8,128)S(1)}, f32[3,7,1024]{2,1,0:T(8,128)S(1)}, u32[]{:S(2)}, u32[]{:S(2)}) collective-permute-start(f32[3,7,1024]{2,1,0:T(8,128)S(1)} %get-tuple-element.51), channel_id=1, source_target_pairs={{0,4},{4,8},{8,12},{12,16},{16,20},{20,24},{24,28},{28,0},{1,5},{5... | collective-permute-start | bytes 258056 | tf_op jit(solution)/shard_map/ppermute | solution.py:19
  9.7 6.1 %collective-permute-start.1 = (f32[3,7,1024]{2,1,0:T(8,128)S(1)}, f32[3,7,1024]{2,1,0:T(8,128)S(1)}, u32[]{:S(2)}, u32[]{:S(2)}) collective-permute-start(f32[3,7,1024]{2,1,0:T(8,128)S(1)} %get-tuple-element.52), channel_id=1, source_target_pairs={{4,0},{8,4},{12,8},{16,12},{20,16},{24,20},{28,24},{0,28},{5,1},{9... | collective-permute-start | bytes 258056 | tf_op jit(solution)/shard_map/ppermute | solution.py:22
  16.0 11.6 %collective-permute-start.3 = (f32[3,46,7]{2,1,0:T(8,128)S(1)}, f32[3,46,7]{2,1,0:T(8,128)S(1)}, u32[]{:S(2)}, u32[]{:S(2)}) collective-permute-start(f32[3,46,7]{2,1,0:T(8,128)S(1)} %get-tuple-element.39), channel_id=1, source_target_pairs={{1,0},{2,1},{3,2},{0,3},{5,4},{6,5},{7,6},{4,7},{9,8},{10,9},{11,1... | collective-permute-start | bytes 11600 | tf_op jit(solution)/shard_map/ppermute | solution.py:22
  19.3 8.2 %collective-permute-start.2 = (f32[3,46,7]{2,1,0:T(8,128)S(1)}, f32[3,46,7]{2,1,0:T(8,128)S(1)}, u32[]{:S(2)}, u32[]{:S(2)}) collective-permute-start(f32[3,46,7]{2,1,0:T(8,128)S(1)} %get-tuple-element.40), channel_id=1, source_target_pairs={{0,1},{1,2},{2,3},{3,0},{4,5},{5,6},{6,7},{7,4},{8,9},{9,10},{10,1... | collective-permute-start | bytes 11600 | tf_op jit(solution)/shard_map/ppermute | solution.py:19
  19.4 4.7 %collective-permute-start.7 = (f32[2,1,46,7]{3,2,1,0:T(8,128)S(1)}, f32[2,1,46,7]{3,2,1,0:T(8,128)S(1)}, u32[]{:S(2)}, u32[]{:S(2)}) collective-permute-start(f32[2,1,46,7]{3,2,1,0:T(8,128)S(1)} %get-tuple-element.53), channel_id=1, source_target_pairs={{1,0},{2,1},{3,2},{0,3},{5,4},{6,5},{7,6},{4,7},{9,8},{10,9},{11,1... | collective-permute-start | bytes 7736 | tf_op jit(solution)/shard_map/ppermute | solution.py:22
  22.4 5.0 %collective-permute-start.6 = (f32[2,1,46,7]{3,2,1,0:T(8,128)S(1)}, f32[2,1,46,7]{3,2,1,0:T(8,128)S(1)}, u32[]{:S(2)}, u32[]{:S(2)}) collective-permute-start(f32[2,1,46,7]{3,2,1,0:T(8,128)S(1)} %get-tuple-element.54), channel_id=1, source_target_pairs={{0,1},{1,2},{2,3},{3,0},{4,5},{5,6},{6,7},{7,4},{8,9},{9,10},{10,1... | collective-permute-start | bytes 7736 | tf_op jit(solution)/shard_map/ppermute | solution.py:19
  33.3 4.3 %copy-start.2 = (f32[34,1026]{1,0:T(8,128)}, f32[34,1026]{1,0:T(8,128)S(1)}, u32[]{:S(2)}) copy-start(f32[34,1026]{1,0:T(8,128)S(1)} %slice.944) | copy-start | bytes 418612
  33.4 2.3 %copy-start.6 = (f32[38,1030]{1,0:T(8,128)}, f32[38,1030]{1,0:T(8,128)S(1)}, u32[]{:S(2)}) copy-start(f32[38,1030]{1,0:T(8,128)S(1)} %slice.914) | copy-start | bytes 469684
  33.6 3.0 %copy-start.4 = (f32[36,1028]{1,0:T(8,128)}, f32[36,1028]{1,0:T(8,128)S(1)}, u32[]{:S(2)}) copy-start(f32[36,1028]{1,0:T(8,128)S(1)} %slice.928) | copy-start | bytes 444100
  79.2 5.5 %collective-permute-start.8 = (f32[2,1,7,1024]{3,2,1,0:T(8,128)S(1)}, f32[2,1,7,1024]{3,2,1,0:T(8,128)S(1)}, u32[]{:S(2)}, u32[]{:S(2)}) collective-permute-start(f32[2,1,7,1024]{3,2,1,0:T(8,128)S(1)} %get-tuple-element.75), channel_id=1, source_target_pairs={{0,4},{4,8},{8,12},{12,16},{16,20},{20,24},{24,28},{28,0},{1,5},{5... | collective-permute-start | bytes 172040 | tf_op jit(solution)/shard_map/ppermute | solution.py:19
  79.3 5.5 %collective-permute-start.9 = (f32[2,1,7,1024]{3,2,1,0:T(8,128)S(1)}, f32[2,1,7,1024]{3,2,1,0:T(8,128)S(1)}, u32[]{:S(2)}, u32[]{:S(2)}) collective-permute-start(f32[2,1,7,1024]{3,2,1,0:T(8,128)S(1)} %get-tuple-element.76), channel_id=1, source_target_pairs={{4,0},{8,4},{12,8},{16,12},{20,16},{24,20},{28,24},{0,28},{5,1},{9... | collective-permute-start | bytes 172040 | tf_op jit(solution)/shard_map/ppermute | solution.py:22
  84.9 8.4 %collective-permute-start.11 = (f32[2,1,46,7]{3,2,1,0:T(8,128)S(1)}, f32[2,1,46,7]{3,2,1,0:T(8,128)S(1)}, u32[]{:S(2)}, u32[]{:S(2)}) collective-permute-start(f32[2,1,46,7]{3,2,1,0:T(8,128)S(1)} %get-tuple-element.49), channel_id=1, source_target_pairs={{1,0},{2,1},{3,2},{0,3},{5,4},{6,5},{7,6},{4,7},{9,8},{10,9},{11,1... | collective-permute-start | bytes 7736 | tf_op jit(solution)/shard_map/ppermute | solution.py:22
  87.4 6.5 %collective-permute-start.10 = (f32[2,1,46,7]{3,2,1,0:T(8,128)S(1)}, f32[2,1,46,7]{3,2,1,0:T(8,128)}, u32[]{:S(2)}, u32[]{:S(2)}) collective-permute-start(f32[2,1,46,7]{3,2,1,0:T(8,128)S(1)} %get-tuple-element.50), channel_id=1, source_target_pairs={{0,1},{1,2},{2,3},{3,0},{4,5},{5,6},{6,7},{7,4},{8,9},{9,10},{10,1... | collective-permute-start | bytes 7736 | tf_op jit(solution)/shard_map/ppermute | solution.py:19
  96.3 1.5 copy-start.9
  96.3 1.5 copy-start.11
  96.3 1.5 copy-start.13
  96.3 1.5 copy-start.15
  96.4 1.5 copy-start.17
  97.8 1.4 copy-start.7
  97.8 1.4 copy-start.35
  97.8 1.4 copy-start.37
  99.2 1.4 copy-start.5
  99.2 1.4 copy-start.19
  99.2 1.4 copy-start.21
  99.3 1.4 copy-start.23
  99.3 1.4 copy-start.25
  (35 other events, 34.8 us)
where the time goes:
time: 154 us
  blocking collectives  77.4 us (50%)
  other arithmetic  23.4 us (15%)
  local copies, waits for them, and re-layouts  21.2 us (14%)
  starting transfers between devices  20.6 us (13%)
  waiting for transfers between devices  6.73 us (4%)
  between operations  4.29 us (3%)
    psum x2, blocking collectives, per_device(): term_total, state_total = lax.psum((term_local, state_local), ('gx', 'gy'))  77.4 us
    ppermute x6, starting transfers between devices, padded(): lax.ppermute(lax.slice_in_dim(block, 0, width, axis=dim), axis, backward)  19.9 us
    another operation x2, local copies, waits for them, and re-layouts, per_device(): jnp.stack([jnp.sum(vector * vector, axis=(0, 2, 3)) for vector in chebysh...  10.4 us
    reduce_sum x12, other arithmetic, per_device(): jnp.sum(vector * vector, axis=(0, 2, 3))  9.75 us
    sub x10, other arithmetic, per_device(): following = 2.0 * applied - shrink(previous, previous_margin - margin + 1)  5.76 us
    ppermute x6, waiting for transfers between devices, padded(): lax.ppermute(lax.slice_in_dim(block, block.shape[dim] - width, None, axis...  4.9 us
    unnamed x110, local copies, waits for them, and re-layouts  3.2 us
  transfers between devices with their start and end apart: 12, of which 4 were waited for; matrix products, arithmetic and copies ran while one was open for 5% of the time, Pallas kernels for 0%

commit v1 on v0

--- a/solution.py
+++ b/solution.py
@@ -115,7 +115,7 @@
             accumulate = accumulate + weights[degree] * jnp.stack([real_rot, imag_rot])
         term_local = jnp.stack([jnp.sum(vector * vector, axis=(0, 2, 3)) for vector in chebyshev])
         state_local = jnp.sum(accumulate * accumulate, axis=(0, 2, 3))
-        term_total, state_total = lax.psum((term_local, state_local), ("gx", "gy"))
+        term_total, state_total = lax.psum(lax.psum((term_local, state_local), "gx"), "gy")
         norm_rows.append(term_total / cell_count)
         rescale = lax.rsqrt(state_total / cell_count + epsilon)
         packet_state = accumulate * rescale[None, :, None, None]

time: 154 us -> 126 us (0.82)
  blocking collectives: 77.4 us -> 51.3 us
  local copies, waits for them, and re-layouts: 21.2 us -> 19.6 us
    psum x2 -> x4, blocking collectives: 77.4 us -> 51.3 us  [the longest x2 32.2 us: per_device(): lax.psum((term_local, state_local), 'gx')]
    unnamed x110 -> x116, local copies, waits for them, and re-layouts: 3.2 us -> 2.61 us
  transfers between devices with their start and end apart: 12 -> 12, of which waited for: 4 -> 4; matrix products, arithmetic and copies ran while one was open for 5% -> 6% of each run, Pallas kernels for 0% -> 0%
where the time goes in v1:
time: 126 us; the launch traced here: 125 us
  blocking collectives  51.3 us (41%)
  other arithmetic  23.2 us (18%)
  starting transfers between devices  20.1 us (16%)
  local copies, waits for them, and re-layouts  19.6 us (16%)
  waiting for transfers between devices  6.77 us (5%)
  between operations  4.27 us (3%)
    psum x2, blocking collectives, per_device(): lax.psum((term_local, state_local), 'gx')  32.2 us
    psum x2, blocking collectives, per_device(): lax.psum(lax.psum((term_local, state_local), 'gx'), 'gy')  19.1 us
    ppermute x6, starting transfers between devices, padded(): lax.ppermute(lax.slice_in_dim(block, 0, width, axis=dim), axis, backward)  19 us
    another operation x2, local copies, waits for them, and re-layouts, per_device(): jnp.stack([jnp.sum(vector * vector, axis=(0, 2, 3)) for vector in chebysh...  10.2 us
    reduce_sum x12, other arithmetic, per_device(): jnp.sum(vector * vector, axis=(0, 2, 3))  9.57 us
    sub x10, other arithmetic, per_device(): following = 2.0 * applied - shrink(previous, previous_margin - margin + 1)  5.79 us
    ppermute x6, waiting for transfers between devices, padded(): lax.ppermute(lax.slice_in_dim(block, block.shape[dim] - width, None, axis...  4.94 us
    unnamed x116, local copies, waits for them, and re-layouts  2.61 us
  transfers between devices with their start and end apart: 12, of which 4 were waited for; matrix products, arithmetic and copies ran while one was open for 6% of the time, Pallas kernels for 0%

profile of v1, /device:TPU:0, one launch (start us, length us, event | category | flops | bytes accessed | tf_op | source)
XLA Modules:
  0.0 125.3 jit_solution(16732381460535738034)
XLA Ops:
  0.7 1.3 %fusion.128 = (s32[1,1]{1,0:T(1,128)}, s32[1,1]{1,0:T(1,128)}) fusion(s32[1,2]{1,0:T(1,128)} %param.14), kind=kLoop, calls=%fused_computation.302 | loop fusion | bytes 16 | tf_op jit(solution)/shard_map/slice | solution.py:89
  3.3 1.1 multiply_bitcast_fusion
  5.0 4.1 %collective-permute-start.5 = (f32[2,1,7,1024]{3,2,1,0:T(8,128)S(1)}, f32[2,1,7,1024]{3,2,1,0:T(8,128)S(1)}, u32[]{:S(2)}, u32[]{:S(2)}) collective-permute-start(f32[2,1,7,1024]{3,2,1,0:T(8,128)S(1)} %get-tuple-element.83), channel_id=1, source_target_pairs={{4,0},{8,4},{12,8},{16,12},{20,16},{24,20},{28,24},{0,28},{5,1},{9... | collective-permute-start | bytes 172040 | tf_op jit(solution)/shard_map/ppermute | solution.py:22
  9.7 3.5 %collective-permute-start.1 = (f32[3,7,1024]{2,1,0:T(8,128)S(1)}, f32[3,7,1024]{2,1,0:T(8,128)S(1)}, u32[]{:S(2)}, u32[]{:S(2)}) collective-permute-start(f32[3,7,1024]{2,1,0:T(8,128)S(1)} %get-tuple-element.55), channel_id=1, source_target_pairs={{4,0},{8,4},{12,8},{16,12},{20,16},{24,20},{28,24},{0,28},{5,1},{9... | collective-permute-start | bytes 258056 | tf_op jit(solution)/shard_map/ppermute | solution.py:22
  16.0 3.4 %collective-permute-start.3 = (f32[3,46,7]{2,1,0:T(8,128)S(1)}, f32[3,46,7]{2,1,0:T(8,128)S(1)}, u32[]{:S(2)}, u32[]{:S(2)}) collective-permute-start(f32[3,46,7]{2,1,0:T(8,128)S(1)} %get-tuple-element.42), channel_id=1, source_target_pairs={{1,0},{2,1},{3,2},{0,3},{5,4},{6,5},{7,6},{4,7},{9,8},{10,9},{11,1... | collective-permute-start | bytes 11600 | tf_op jit(solution)/shard_map/ppermute | solution.py:22
  19.4 2.9 %collective-permute-start.7 = (f32[2,1,46,7]{3,2,1,0:T(8,128)S(1)}, f32[2,1,46,7]{3,2,1,0:T(8,128)S(1)}, u32[]{:S(2)}, u32[]{:S(2)}) collective-permute-start(f32[2,1,46,7]{3,2,1,0:T(8,128)S(1)} %get-tuple-element.56), channel_id=1, source_target_pairs={{1,0},{2,1},{3,2},{0,3},{5,4},{6,5},{7,6},{4,7},{9,8},{10,9},{11,1... | collective-permute-start | bytes 7736 | tf_op jit(solution)/shard_map/ppermute | solution.py:22
  22.4 1.8 %collective-permute-done.7 = f32[2,1,46,7]{3,2,1,0:T(8,128)S(1)} collective-permute-done((f32[2,1,46,7]{3,2,1,0:T(8,128)S(1)}, f32[2,1,46,7]{3,2,1,0:T(8,128)S(1)}, u32[]{:S(2)}, u32[]{:S(2)}) %collective-permute-start.7) | collective-permute-done | bytes 2608 | tf_op jit(solution)/shard_map/ppermute | solution.py:22
  24.2 3.2 %collective-permute-done.6 = f32[2,1,46,7]{3,2,1,0:T(8,128)S(1)} collective-permute-done((f32[2,1,46,7]{3,2,1,0:T(8,128)S(1)}, f32[2,1,46,7]{3,2,1,0:T(8,128)S(1)}, u32[]{:S(2)}, u32[]{:S(2)}) %collective-permute-start.6) | collective-permute-done | bytes 2608 | tf_op jit(solution)/shard_map/ppermute | solution.py:19
  30.3 0.8 fusion.65
  38.0 1.1 multiply_reduce_fusion.5
  39.2 0.9 multiply_reduce_fusion.11
  40.0 15.0 %psum.56 = f32[1]{0:T(128)} all-reduce(f32[1]{0:T(128)} %bitcast.29), channel_id=1, replica_groups=mesh['gx'=8,'gy'=4] {'gx'}, use_global_device_ids=true, to_apply=%region_3.4 | all-reduce | flops 1 | bytes 8 | tf_op jit(solution)/shard_map/psum | solution.py:118
  55.0 0.7 fusion.64
  55.8 8.5 %psum.57 = f32[1]{0:T(128)} all-reduce(f32[1]{0:T(128)} %psum.56), channel_id=1, replica_groups=mesh['gx'=8,'gy'=4] {'gy'}, use_global_device_ids=true, to_apply=%region_4.5 | all-reduce | flops 1 | bytes 8 | tf_op jit(solution)/shard_map/psum | solution.py:118
  65.0 0.7 multiply_reduce_fusion.4
  65.8 3.5 %collective-permute-start.9 = (f32[2,1,7,1024]{3,2,1,0:T(8,128)S(1)}, f32[2,1,7,1024]{3,2,1,0:T(8,128)S(1)}, u32[]{:S(2)}, u32[]{:S(2)}) collective-permute-start(f32[2,1,7,1024]{3,2,1,0:T(8,128)S(1)} %get-tuple-element.79), channel_id=1, source_target_pairs={{4,0},{8,4},{12,8},{16,12},{20,16},{24,20},{28,24},{0,28},{5,1},{9... | collective-permute-start | bytes 172040 | tf_op jit(solution)/shard_map/ppermute | solution.py:22
  69.3 0.8 fusion.63
  70.1 1.2 collective-permute-done.8
  71.4 1.6 %collective-permute-start.11 = (f32[2,1,46,7]{3,2,1,0:T(8,128)S(1)}, f32[2,1,46,7]{3,2,1,0:T(8,128)S(1)}, u32[]{:S(2)}, u32[]{:S(2)}) collective-permute-start(f32[2,1,46,7]{3,2,1,0:T(8,128)S(1)} %get-tuple-element.52), channel_id=1, source_target_pairs={{1,0},{2,1},{3,2},{0,3},{5,4},{6,5},{7,6},{4,7},{9,8},{10,9},{11,1... | collective-permute-start | bytes 7736 | tf_op jit(solution)/shard_map/ppermute | solution.py:22
  73.4 0.7 multiply_reduce_fusion.8
  74.1 5.1 %stack.171 = f32[8,1]{0,1:T(1,128)S(1)} concatenate(f32[1,1]{0,1:T(1,128)} %bitcast.35, f32[1,1]{0,1:T(1,128)} %bitcast.36, f32[1,1]{0,1:T(1,128)} %bitcast.37, f32[1,1]{0,1:T(1,128)} %bitcast.38, f32[1,1]{0,1:T(1,128)} %bitcast.39, f32[1,1]{0,1:T(1,128)} %bitcast.40, f32[1,1]{0,1:T(1,128)} %bitcast.41, f32[1,1]{0,1:T(1,128)} %bitcast.42), dimensions={0} | concatenate | bytes 64 | tf_op jit(solution)/shard_map/stack | solution.py:116
  80.0 0.7 fusion.62
  80.8 0.7 slice_subtract_fusion
  81.5 0.8 fusion.61
  82.9 0.8 fusion.60
  84.3 0.8 multiply_reduce_fusion.3
  88.1 1.0 multiply_reduce_fusion
  89.6 5.2 %stack.181 = f32[8,1]{0,1:T(1,128)S(1)} concatenate(f32[1,1]{0,1:T(1,128)} %bitcast.44, f32[1,1]{0,1:T(1,128)} %bitcast.45, f32[1,1]{0,1:T(1,128)} %bitcast.46, f32[1,1]{0,1:T(1,128)} %bitcast.47, f32[1,1]{0,1:T(1,128)} %bitcast.48, f32[1,1]{0,1:T(1,128)} %bitcast.49, f32[1,1]{0,1:T(1,128)} %bitcast.50, f32[1,1]{0,1:T(1,128)} %bitcast.51), dimensions={0} | concatenate | bytes 64 | tf_op jit(solution)/shard_map/stack | solution.py:116
  94.7 0.8 multiply_reduce_fusion.10
  95.5 17.2 %all-reduce = (f32[1]{0:T(128)}, f32[8,1]{0,1:T(1,128)S(1)}, f32[8,1]{0,1:T(1,128)S(1)}) all-reduce(f32[1]{0:T(128)} %bitcast.31, f32[8,1]{0,1:T(1,128)S(1)} %stack.181, f32[8,1]{0,1:T(1,128)S(1)} %stack.171), channel_id=1, replica_groups=mesh['gx'=8,'gy'=4] {'gx'}, use_global_device_ids=true, to_apply=%region_6.7 | all-reduce | flops 17 | bytes 136 | tf_op jit(solution)/shard_map/psum | solution.py:118
  112.7 10.5 %all-reduce.1 = (f32[1]{0:T(128)}, f32[8,1]{0,1:T(1,128)S(1)}, f32[8,1]{0,1:T(1,128)S(1)}) all-reduce(f32[1]{0:T(128)} %get-tuple-element.5, f32[8,1]{0,1:T(1,128)S(1)} %get-tuple-element.6, f32[8,1]{0,1:T(1,128)S(1)} %get-tuple-element.7), channel_id=1, replica_groups=mesh['gx'=8,'gy'=4] {'gy'}, use_global_device_ids=true, to_apply=%region_7.8 | all-reduce | flops 17 | bytes 136 | tf_op jit(solution)/shard_map/psum | solution.py:118
  124.0 0.7 slice_bitcast_fusion.21
  (195 shorter events, 20.0 us)
Async XLA Ops:
  0.6 8.4 %copy-start.57 = (f32[16]{0:T(128)S(1)}, f32[16]{0:T(128)}, u32[]{:S(2)}) copy-start(f32[16]{0:T(128)} %param.13) | copy-start | bytes 196
  0.6 8.4 %copy-start.56 = (s32[32,1024]{1,0:T(8,128)S(1)}, s32[32,1024]{1,0:T(8,128)}, u32[]{:S(2)}) copy-start(s32[32,1024]{1,0:T(8,128)} %param.12) | copy-start | bytes 393220
  0.7 8.4 %copy-start.55 = (s32[32,1024]{1,0:T(8,128)S(1)}, s32[32,1024]{1,0:T(8,128)}, u32[]{:S(2)}) copy-start(s32[32,1024]{1,0:T(8,128)} %param.11) | copy-start | bytes 393220
  3.3 6.3 %copy-start.54 = (f32[32,1024]{1,0:T(8,128)S(1)}, f32[32,1024]{1,0:T(8,128)}, u32[]{:S(2)}) copy-start(f32[32,1024]{1,0:T(8,128)} %param.10) | copy-start | bytes 393220
  4.4 10.7 %collective-permute-start.4 = (f32[2,1,7,1024]{3,2,1,0:T(8,128)S(1)}, f32[2,1,7,1024]{3,2,1,0:T(8,128)S(1)}, u32[]{:S(2)}, u32[]{:S(2)}) collective-permute-start(f32[2,1,7,1024]{3,2,1,0:T(8,128)S(1)} %get-tuple-element.82), channel_id=1, source_target_pairs={{0,4},{4,8},{8,12},{12,16},{16,20},{20,24},{24,28},{28,0},{1,5},{5... | collective-permute-start | bytes 172040 | tf_op jit(solution)/shard_map/ppermute | solution.py:19
  5.0 10.2 %collective-permute-start.5 = (f32[2,1,7,1024]{3,2,1,0:T(8,128)S(1)}, f32[2,1,7,1024]{3,2,1,0:T(8,128)S(1)}, u32[]{:S(2)}, u32[]{:S(2)}) collective-permute-start(f32[2,1,7,1024]{3,2,1,0:T(8,128)S(1)} %get-tuple-element.83), channel_id=1, source_target_pairs={{4,0},{8,4},{12,8},{16,12},{20,16},{24,20},{28,24},{0,28},{5,1},{9... | collective-permute-start | bytes 172040 | tf_op jit(solution)/shard_map/ppermute | solution.py:22
  9.6 6.2 %collective-permute-start = (f32[3,7,1024]{2,1,0:T(8,128)S(1)}, f32[3,7,1024]{2,1,0:T(8,128)S(1)}, u32[]{:S(2)}, u32[]{:S(2)}) collective-permute-start(f32[3,7,1024]{2,1,0:T(8,128)S(1)} %get-tuple-element.54), channel_id=1, source_target_pairs={{0,4},{4,8},{8,12},{12,16},{16,20},{20,24},{24,28},{28,0},{1,5},{5... | collective-permute-start | bytes 258056 | tf_op jit(solution)/shard_map/ppermute | solution.py:19
  9.7 6.1 %collective-permute-start.1 = (f32[3,7,1024]{2,1,0:T(8,128)S(1)}, f32[3,7,1024]{2,1,0:T(8,128)S(1)}, u32[]{:S(2)}, u32[]{:S(2)}) collective-permute-start(f32[3,7,1024]{2,1,0:T(8,128)S(1)} %get-tuple-element.55), channel_id=1, source_target_pairs={{4,0},{8,4},{12,8},{16,12},{20,16},{24,20},{28,24},{0,28},{5,1},{9... | collective-permute-start | bytes 258056 | tf_op jit(solution)/shard_map/ppermute | solution.py:22
  16.0 11.6 %collective-permute-start.3 = (f32[3,46,7]{2,1,0:T(8,128)S(1)}, f32[3,46,7]{2,1,0:T(8,128)S(1)}, u32[]{:S(2)}, u32[]{:S(2)}) collective-permute-start(f32[3,46,7]{2,1,0:T(8,128)S(1)} %get-tuple-element.42), channel_id=1, source_target_pairs={{1,0},{2,1},{3,2},{0,3},{5,4},{6,5},{7,6},{4,7},{9,8},{10,9},{11,1... | collective-permute-start | bytes 11600 | tf_op jit(solution)/shard_map/ppermute | solution.py:22
  19.3 8.3 %collective-permute-start.2 = (f32[3,46,7]{2,1,0:T(8,128)S(1)}, f32[3,46,7]{2,1,0:T(8,128)S(1)}, u32[]{:S(2)}, u32[]{:S(2)}) collective-permute-start(f32[3,46,7]{2,1,0:T(8,128)S(1)} %get-tuple-element.43), channel_id=1, source_target_pairs={{0,1},{1,2},{2,3},{3,0},{4,5},{5,6},{6,7},{7,4},{8,9},{9,10},{10,1... | collective-permute-start | bytes 11600 | tf_op jit(solution)/shard_map/ppermute | solution.py:19
  19.4 4.7 %collective-permute-start.7 = (f32[2,1,46,7]{3,2,1,0:T(8,128)S(1)}, f32[2,1,46,7]{3,2,1,0:T(8,128)S(1)}, u32[]{:S(2)}, u32[]{:S(2)}) collective-permute-start(f32[2,1,46,7]{3,2,1,0:T(8,128)S(1)} %get-tuple-element.56), channel_id=1, source_target_pairs={{1,0},{2,1},{3,2},{0,3},{5,4},{6,5},{7,6},{4,7},{9,8},{10,9},{11,1... | collective-permute-start | bytes 7736 | tf_op jit(solution)/shard_map/ppermute | solution.py:22
  22.4 5.0 %collective-permute-start.6 = (f32[2,1,46,7]{3,2,1,0:T(8,128)S(1)}, f32[2,1,46,7]{3,2,1,0:T(8,128)S(1)}, u32[]{:S(2)}, u32[]{:S(2)}) collective-permute-start(f32[2,1,46,7]{3,2,1,0:T(8,128)S(1)} %get-tuple-element.57), channel_id=1, source_target_pairs={{0,1},{1,2},{2,3},{3,0},{4,5},{5,6},{6,7},{7,4},{8,9},{9,10},{10,1... | collective-permute-start | bytes 7736 | tf_op jit(solution)/shard_map/ppermute | solution.py:19
  31.4 5.4 %copy-start.6 = (f32[34,1026]{1,0:T(8,128)}, f32[34,1026]{1,0:T(8,128)S(1)}, u32[]{:S(2)}) copy-start(f32[34,1026]{1,0:T(8,128)S(1)} %slice.944) | copy-start | bytes 418612
  31.5 3.4 %copy-start.10 = (f32[38,1030]{1,0:T(8,128)}, f32[38,1030]{1,0:T(8,128)S(1)}, u32[]{:S(2)}) copy-start(f32[38,1030]{1,0:T(8,128)S(1)} %slice.914) | copy-start | bytes 469684
  31.6 4.1 %copy-start.8 = (f32[36,1028]{1,0:T(8,128)}, f32[36,1028]{1,0:T(8,128)S(1)}, u32[]{:S(2)}) copy-start(f32[36,1028]{1,0:T(8,128)S(1)} %slice.928) | copy-start | bytes 444100
  31.8 6.3 %copy-start.44 = (f32[32,1024]{1,0:T(8,128)}, f32[32,1024]{1,0:T(8,128)S(1)}, u32[]{:S(2)}) copy-start(f32[32,1024]{1,0:T(8,128)S(1)} %slice.960) | copy-start | bytes 393220
  31.9 1.6 %copy-start.12 = (f32[40,1032]{1,0:T(8,128)}, f32[40,1032]{1,0:T(8,128)S(1)}, u32[]{:S(2)}) copy-start(f32[40,1032]{1,0:T(8,128)S(1)} %slice.898) | copy-start | bytes 495364
  65.7 5.5 %collective-permute-start.8 = (f32[2,1,7,1024]{3,2,1,0:T(8,128)S(1)}, f32[2,1,7,1024]{3,2,1,0:T(8,128)S(1)}, u32[]{:S(2)}, u32[]{:S(2)}) collective-permute-start(f32[2,1,7,1024]{3,2,1,0:T(8,128)S(1)} %get-tuple-element.78), channel_id=1, source_target_pairs={{0,4},{4,8},{8,12},{12,16},{16,20},{20,24},{24,28},{28,0},{1,5},{5... | collective-permute-start | bytes 172040 | tf_op jit(solution)/shard_map/ppermute | solution.py:19
  65.8 5.5 %collective-permute-start.9 = (f32[2,1,7,1024]{3,2,1,0:T(8,128)S(1)}, f32[2,1,7,1024]{3,2,1,0:T(8,128)S(1)}, u32[]{:S(2)}, u32[]{:S(2)}) collective-permute-start(f32[2,1,7,1024]{3,2,1,0:T(8,128)S(1)} %get-tuple-element.79), channel_id=1, source_target_pairs={{4,0},{8,4},{12,8},{16,12},{20,16},{24,20},{28,24},{0,28},{5,1},{9... | collective-permute-start | bytes 172040 | tf_op jit(solution)/shard_map/ppermute | solution.py:22
  71.4 7.9 %collective-permute-start.11 = (f32[2,1,46,7]{3,2,1,0:T(8,128)S(1)}, f32[2,1,46,7]{3,2,1,0:T(8,128)S(1)}, u32[]{:S(2)}, u32[]{:S(2)}) collective-permute-start(f32[2,1,46,7]{3,2,1,0:T(8,128)S(1)} %get-tuple-element.52), channel_id=1, source_target_pairs={{1,0},{2,1},{3,2},{0,3},{5,4},{6,5},{7,6},{4,7},{9,8},{10,9},{11,1... | collective-permute-start | bytes 7736 | tf_op jit(solution)/shard_map/ppermute | solution.py:22
  72.9 6.3 %collective-permute-start.10 = (f32[2,1,46,7]{3,2,1,0:T(8,128)S(1)}, f32[2,1,46,7]{3,2,1,0:T(8,128)S(1)}, u32[]{:S(2)}, u32[]{:S(2)}) collective-permute-start(f32[2,1,46,7]{3,2,1,0:T(8,128)S(1)} %get-tuple-element.53), channel_id=1, source_target_pairs={{0,1},{1,2},{2,3},{3,0},{4,5},{5,6},{6,7},{7,4},{8,9},{9,10},{10,1... | collective-permute-start | bytes 7736 | tf_op jit(solution)/shard_map/ppermute | solution.py:19
  80.8 1.5 %copy-start.13 = (f32[40,1032]{1,0:T(8,128)S(1)}, f32[40,1032]{1,0:T(8,128)}, u32[]{:S(2)}) copy-start(f32[40,1032]{1,0:T(8,128)} %copy-done.12) | copy-start | bytes 495364
  80.8 1.5 %copy-start.15 = (f32[40,1032]{1,0:T(8,128)S(1)}, f32[40,1032]{1,0:T(8,128)}, u32[]{:S(2)}) copy-start(f32[40,1032]{1,0:T(8,128)} %copy-done.14) | copy-start | bytes 495364
  80.8 1.5 %copy-start.17 = (f32[40,1032]{1,0:T(8,128)S(1)}, f32[40,1032]{1,0:T(8,128)}, u32[]{:S(2)}) copy-start(f32[40,1032]{1,0:T(8,128)} %copy-done.16) | copy-start | bytes 495364
  80.8 1.5 %copy-start.19 = (f32[40,1032]{1,0:T(8,128)S(1)}, f32[40,1032]{1,0:T(8,128)}, u32[]{:S(2)}) copy-start(f32[40,1032]{1,0:T(8,128)} %copy-done.18) | copy-start | bytes 495364
  82.3 1.4 %copy-start.11 = (f32[38,1030]{1,0:T(8,128)S(1)}, f32[38,1030]{1,0:T(8,128)}, u32[]{:S(2)}) copy-start(f32[38,1030]{1,0:T(8,128)} %copy-done.10) | copy-start | bytes 469684
  82.3 1.4 %copy-start.37 = (f32[38,1030]{1,0:T(8,128)S(1)}, f32[38,1030]{1,0:T(8,128)}, u32[]{:S(2)}) copy-start(f32[38,1030]{1,0:T(8,128)} %copy-done.36) | copy-start | bytes 469684
  82.3 1.4 %copy-start.39 = (f32[38,1030]{1,0:T(8,128)S(1)}, f32[38,1030]{1,0:T(8,128)}, u32[]{:S(2)}) copy-start(f32[38,1030]{1,0:T(8,128)} %copy-done.38) | copy-start | bytes 469684
  83.7 1.4 %copy-start.9 = (f32[36,1028]{1,0:T(8,128)S(1)}, f32[36,1028]{1,0:T(8,128)}, u32[]{:S(2)}) copy-start(f32[36,1028]{1,0:T(8,128)} %copy-done.8) | copy-start | bytes 444100
  83.7 1.4 %copy-start.21 = (f32[36,1028]{1,0:T(8,128)S(1)}, f32[36,1028]{1,0:T(8,128)}, u32[]{:S(2)}) copy-start(f32[36,1028]{1,0:T(8,128)} %copy-done.20) | copy-start | bytes 444100
  83.7 1.4 %copy-start.23 = (f32[36,1028]{1,0:T(8,128)S(1)}, f32[36,1028]{1,0:T(8,128)}, u32[]{:S(2)}) copy-start(f32[36,1028]{1,0:T(8,128)} %copy-done.22) | copy-start | bytes 444100
  83.7 1.4 %copy-start.25 = (f32[36,1028]{1,0:T(8,128)S(1)}, f32[36,1028]{1,0:T(8,128)}, u32[]{:S(2)}) copy-start(f32[36,1028]{1,0:T(8,128)} %copy-done.24) | copy-start | bytes 444100
  (38 other events, 38.3 us)
